TPU v7x, 256 devices: a whole 4x4x8 slice. The times are simulated.
256 devices in a mesh: feat: 32 (over y, z), dp: 8 (over x, core).
Axes of the slice: x: 4, y: 4, z: 8, core: 2. Of those that a mesh axis runs over, the one named last changes fastest.
Arguments:
- face_grid: bfloat16 [32768, 10240], P('dp', 'feat'), may hold values from -6 to 6
- first_nbrs: int32 [16384, 8], P('dp'), may hold values from 0 to 4095
- first_count: int32 [16384], P('dp'), may hold values from 1 to 8
- w_first: bfloat16 [10240, 256], P('feat'), may hold values from -0.0625 to 0.0625
- b_first: float32 [256], replicated, may hold values from -3 to 3
- send_rows: int32 [4096], P('dp'), may hold values from 0 to 2047
- second_nbrs: int32 [16384, 8], P(('dp', 'feat')), may hold values from 0 to 2559
- second_count: int32 [16384], P(('dp', 'feat')), may hold values from 1 to 8
- w_in: bfloat16 [256, 1024], replicated, may hold values from -0.375 to 0.375
- w_out: bfloat16 [1024, 256], replicated, may hold values from -0.1875 to 0.1875
- out_grad: bfloat16 [16384, 256], P(('dp', 'feat')), may hold values from -6 to 6
Outputs:
- embed: bfloat16 [16384, 256], P(('dp', 'feat'))
- grad_first: float32 [10240, 256], P('feat')
Inputs may be any that keep to these rules, and one draw needn't show every extreme that they name: `first_count`: slots at or past a target's count are ignored; counts lie in 1 to 8. `first_nbrs`: only slots below first_count are read. `second_count`: slots at or past a target's count are ignored. `second_nbrs`: indices below 2048 name the partition's own targets, the rest the faces received from the previous partition in order; only slots below second_count are read. `send_rows`: entries may repeat.
All inputs are finite; a program needn't handle non-finite values.
Results may differ from a plain program's by a relative error of at most 0.0061.
Values may be sent and summed in bfloat16 or wider, within the bound.
No kernel may reach another device: no remote copies, remote signals or barrier semaphores. Data moves between devices by JAX's collectives and lax.ppermute only.
A program may use at most 64 MiB of HBM per device.

v0:
```python
import jax
import jax.numpy as jnp
from jax import lax
from jax.sharding import PartitionSpec as P


def passed_along(shard, axis, by):
    devices = lax.axis_size(axis)
    return lax.ppermute(shard, axis, [(i, (i + by) % devices) for i in range(devices)])


def slope(value):
    sig = jax.nn.sigmoid(value)
    return sig * (1.0 + value * (1.0 - sig))


def mean_rows(table, nbrs, count):
    total = jnp.zeros((nbrs.shape[0], table.shape[1]), jnp.float32)
    for slot in range(nbrs.shape[1]):
        picked = table[nbrs[:, slot]].astype(jnp.float32)
        total = total + jnp.where((slot < count)[:, None], picked, 0.0)
    return total / count[:, None].astype(jnp.float32)


def spread(grad, nbrs, count, size):
    slots = jnp.arange(nbrs.shape[1], dtype=jnp.int32)
    factor = jnp.where(
        slots[None, :] < count[:, None], 1.0 / count[:, None].astype(jnp.float32), 0.0
    )
    terms = (grad[:, None, :] * factor[:, :, None]).reshape(-1, grad.shape[1])
    return jax.ops.segment_sum(terms, nbrs.reshape(-1), num_segments=size)


def body(
    face_grid,
    first_nbrs,
    first_count,
    w_first,
    b_first,
    send_rows,
    second_nbrs,
    second_count,
    w_in,
    w_out,
    out_grad,
):
    targets = first_nbrs.shape[0]
    agg_first = (
        face_grid[:targets].astype(jnp.float32) + mean_rows(face_grid, first_nbrs, first_count)
    ).astype(jnp.bfloat16)
    partial_value = jnp.dot(agg_first, w_first, preferred_element_type=jnp.float32)
    pre_own = lax.psum_scatter(partial_value, "feat", scatter_dimension=0, tiled=True) + b_first
    hidden_own = jax.nn.silu(pre_own).astype(jnp.bfloat16)
    table = lax.all_gather(hidden_own, "feat", axis=0, tiled=True)
    received = passed_along(table[send_rows], "dp", 1)
    extended = jnp.concatenate([table, received], axis=0)
    agg_second = (
        hidden_own.astype(jnp.float32) + mean_rows(extended, second_nbrs, second_count)
    ).astype(jnp.bfloat16)
    pre_mlp = jnp.dot(agg_second, w_in, preferred_element_type=jnp.float32)
    act_mlp = jax.nn.silu(pre_mlp).astype(jnp.bfloat16)
    embed = (
        hidden_own.astype(jnp.float32) + jnp.dot(act_mlp, w_out, preferred_element_type=jnp.float32)
    ).astype(jnp.bfloat16)
    grad_act = lax.dot_general(
        out_grad, w_out, (((1,), (1,)), ((), ())), preferred_element_type=jnp.float32
    )
    grad_pre_mlp = (grad_act * slope(pre_mlp)).astype(jnp.bfloat16)
    grad_agg = lax.dot_general(
        grad_pre_mlp, w_in, (((1,), (1,)), ((), ())), preferred_element_type=jnp.float32
    )
    grad_ext = spread(grad_agg, second_nbrs, second_count, extended.shape[0])
    full_rows = table.shape[0]
    returned = passed_along(grad_ext[full_rows:].astype(jnp.bfloat16), "dp", -1).astype(jnp.float32)
    table_grad = grad_ext[:full_rows].at[send_rows].add(returned)
    own_terms = out_grad.astype(jnp.float32) + grad_agg
    grad_own = (
        lax.psum_scatter(
            table_grad.astype(jnp.bfloat16), "feat", scatter_dimension=0, tiled=True
        ).astype(jnp.float32)
        + own_terms
    )
    grad_pre_own = (grad_own * slope(pre_own)).astype(jnp.bfloat16)
    grad_pre_first = lax.all_gather(grad_pre_own, "feat", axis=0, tiled=True)
    slice_grad = lax.dot_general(
        agg_first, grad_pre_first, (((0,), (0,)), ((), ())), preferred_element_type=jnp.float32
    )
    grad_first = lax.psum(slice_grad, "dp")
    return (embed, grad_first)


def solution(mesh):
    return jax.shard_map(
        body,
        mesh=mesh,
        in_specs=(
            P("dp", "feat"),
            P("dp", None),
            P("dp"),
            P("feat", None),
            P(),
            P("dp"),
            P(("dp", "feat"), None),
            P(("dp", "feat")),
            P(),
            P(),
            P(("dp", "feat"), None),
        ),
        out_specs=(P(("dp", "feat"), None), P("feat", None)),
        check_vma=False,
    )
```

profile of v0, /device:TPU:8, one launch (start us, length us, event | category | flops | bytes accessed | tf_op | source)
XLA Modules:
  0.0 828.4 jit_solution(5859287706951482798)
XLA Ops:
  7.2 0.0 copy-start
  7.2 0.0 reduce-scatter.3.cloned.1.call-start
  7.2 0.8 broadcast_compare_fusion.7
  8.0 0.7 convert_element_type.107
  8.7 4.6 copy.22
  13.3 0.0 copy-done.5
  13.3 0.1 compare_select_fusion.7
  13.4 11.2 %gather_fusion = bf16[2048,320]{1,0:T(8,128)(2,1)} fusion(bf16[4096,320]{1,0:T(8,128)(2,1)} %copy.22, s32[2048]{0:T(1024)S(1)} %broadcast_clamp_fusion.7), kind=kCustom, calls=%fused_computation | custom fusion | bytes 2629632 | tf_op jit(solution)/shard_map/gather | solution.py:20
  24.6 11.2 %gather_fusion.1 = bf16[2048,320]{1,0:T(8,128)(2,1)} fusion(bf16[4096,320]{1,0:T(8,128)(2,1)} %copy.22, s32[2048]{0:T(1024)S(1)} %broadcast_clamp_fusion.6), kind=kCustom, calls=%fused_computation.1 | custom fusion | bytes 2629632 | tf_op jit(solution)/shard_map/gather | solution.py:20
  35.8 11.2 %gather_fusion.2 = bf16[2048,320]{1,0:T(8,128)(2,1)} fusion(bf16[4096,320]{1,0:T(8,128)(2,1)} %copy.22, s32[2048]{0:T(1024)S(1)} %broadcast_clamp_fusion.5), kind=kCustom, calls=%fused_computation.2 | custom fusion | bytes 2629632 | tf_op jit(solution)/shard_map/gather | solution.py:20
  47.0 11.2 %gather_fusion.3 = bf16[2048,320]{1,0:T(8,128)(2,1)} fusion(bf16[4096,320]{1,0:T(8,128)(2,1)} %copy.22, s32[2048]{0:T(1024)S(1)} %broadcast_clamp_fusion.4), kind=kCustom, calls=%fused_computation.3 | custom fusion | bytes 2629632 | tf_op jit(solution)/shard_map/gather | solution.py:20
  58.1 11.2 %gather_fusion.4 = bf16[2048,320]{1,0:T(8,128)(2,1)} fusion(bf16[4096,320]{1,0:T(8,128)(2,1)} %copy.22, s32[2048]{0:T(1024)S(1)} %broadcast_clamp_fusion.3), kind=kCustom, calls=%fused_computation.4 | custom fusion | bytes 2629632 | tf_op jit(solution)/shard_map/gather | solution.py:20
  69.3 11.2 %gather_fusion.5 = bf16[2048,320]{1,0:T(8,128)(2,1)} fusion(bf16[4096,320]{1,0:T(8,128)(2,1)} %copy.22, s32[2048]{0:T(1024)S(1)} %broadcast_clamp_fusion.2), kind=kCustom, calls=%fused_computation.5 | custom fusion | bytes 2629632 | tf_op jit(solution)/shard_map/gather | solution.py:20
  80.5 11.2 %gather_fusion.6 = bf16[2048,320]{1,0:T(8,128)(2,1)} fusion(bf16[4096,320]{1,0:T(8,128)(2,1)} %copy.22, s32[2048]{0:T(1024)S(1)} %broadcast_clamp_fusion.1), kind=kCustom, calls=%fused_computation.6 | custom fusion | bytes 2629632 | tf_op jit(solution)/shard_map/gather | solution.py:20
  91.7 11.2 %gather_fusion.7 = bf16[2048,320]{1,0:T(8,128)(2,1)} fusion(bf16[4096,320]{1,0:T(8,128)(2,1)} %copy.22, s32[2048]{0:T(1024)S(1)} %broadcast_clamp_fusion), kind=kCustom, calls=%fused_computation.7 | custom fusion | bytes 2629632 | tf_op jit(solution)/shard_map/gather | solution.py:20
  102.8 8.9 %add_convert_fusion = bf16[2048,320]{1,0:T(8,128)(2,1)S(1)} fusion(bf16[2048,320]{1,0:T(8,128)(2,1)} %gather_fusion.7, bf16[2048,320]{1,0:T(8,128)(2,1)} %gather_fusion.6, bf16[2048,320]{1,0:T(8,128)(2,1)} %gather_fusion.5, bf16[2048,320]{1,0:T(8,128)(2,1)} %gather_fusion.4, bf16[2048,320]{1,0:T(8,128)(2,1)} %gather_fusion.3, ...), kind=kLoop, calls=%fused_computation.19 | loop fusion | flops 17694720 | bytes 13131776 | tf_op jit(solution)/shard_map/convert_element_type | solution.py:50
  111.8 2.0 fusion.40
  113.8 0.0 reduce-scatter.3.cloned.1.call-update
  113.8 0.0 all-gather.3.cloned.1.call-start
  113.9 220.8 %reduce-scatter.3.cloned.1.call-done = f32[64,256]{1,0:T(8,128)} async-done(((f32[2048,256]{1,0:T(8,128)}), f32[64,256]{1,0:T(8,128)}) %reduce-scatter.3.cloned.1.call-update) | async-done | bytes 65552 | tf_op jit(solution)/shard_map/reduce_scatter | solution.py:52
  334.7 1.5 multiply_convert_fusion.3
  336.2 0.0 all-gather.3.cloned.1.call-update
  336.2 0.2 reduce-scatter.5.cloned.1.call-start
  336.6 0.1 fusion.28
  336.6 75.6 %all-gather.3.cloned.1.call-done = bf16[2048,256]{1,0:T(8,128)(2,1)} async-done(((bf16[64,256]{1,0:T(8,128)(2,1)}), bf16[2048,256]{1,0:T(8,128)(2,1)}) %all-gather.3.cloned.1.call-update) | async-done | bytes 1048592 | tf_op jit(solution)/shard_map/all_gather | solution.py:54
  412.2 3.6 gather_fusion.8
  415.9 0.0 collective-permute-start
  415.9 0.1 copy.31
  416.0 0.1 select_n.163
  416.1 0.1 reshape.203
  416.2 1.1 constant_dynamic-update-slice_fusion.1
  417.3 5.8 collective-permute-done
  423.1 0.7 constant_dynamic-update-slice_fusion
  423.8 2.1 gather_fusion.10
  426.0 0.0 copy-start.6
  426.0 0.0 copy-start.11
  426.0 2.2 gather_fusion.11
  428.2 2.1 gather_fusion.12
  430.3 2.1 gather_fusion.13
  432.5 2.1 gather_fusion.14
  434.6 2.1 gather_fusion.15
  436.8 2.1 gather_fusion.9
  438.9 2.1 gather_fusion.16
  441.1 0.3 fusion.16
  441.4 0.5 fusion.3
  441.9 5.1 scatter_custom_fusion
  447.0 1.1 slice.132
  448.0 0.0 collective-permute-start.1
  448.1 3.1 slice.112
  451.2 0.8 collective-permute-done.1
  451.9 6.0 scatter_custom_fusion.1
  457.9 2.7 convert_element_type.125
  460.6 0.0 reduce-scatter.5.cloned.1.call-update
  460.7 0.0 all-gather.5.cloned.1.call-start
  460.7 215.0 %reduce-scatter.5.cloned.1.call-done = bf16[64,256]{1,0:T(8,128)(2,1)} async-done(((bf16[2048,256]{1,0:T(8,128)(2,1)}), bf16[64,256]{1,0:T(8,128)(2,1)}) %reduce-scatter.5.cloned.1.call-update) | async-done | bytes 32784 | tf_op jit(solution)/shard_map/reduce_scatter | solution.py:78
  675.8 1.4 multiply_convert_fusion.2
  677.2 0.0 all-gather.5.cloned.1.call-update
  677.2 0.0 all-reduce.2.cloned.1.call-start
  677.2 75.9 %all-gather.5.cloned.1.call-done = bf16[2048,256]{1,0:T(8,128)(2,1)} async-done(((bf16[64,256]{1,0:T(8,128)(2,1)}), bf16[2048,256]{1,0:T(8,128)(2,1)}) %all-gather.5.cloned.1.call-update) | async-done | bytes 1048592 | tf_op jit(solution)/shard_map/all_gather | solution.py:84
  753.1 2.5 fusion.41
  755.7 0.0 all-reduce.2.cloned.1.call-update
  755.7 0.8 fusion.4
  756.6 63.6 %all-reduce.2.cloned.1.call-done = f32[320,256]{1,0:T(8,128)} async-done(((f32[320,256]{1,0:T(8,128)}), f32[320,256]{1,0:T(8,128)}) %all-reduce.2.cloned.1.call-update) | async-done | bytes 327696 | tf_op jit(solution)/shard_map/psum | solution.py:88
  820.1 1.7 copy.35
  (38 shorter events, 0.1 us)
Async XLA Ops:
  7.2 433.9 %copy-start = (bf16[256,1024]{1,0:T(8,128)(2,1)S(1)}, bf16[256,1024]{1,0:T(8,128)(2,1)}, u32[]{:S(2)}) copy-start(bf16[256,1024]{1,0:T(8,128)(2,1)} %param.19) | copy-start | bytes 1572868
  7.2 327.5 %reduce-scatter.3.cloned.1.call-start = ((), (), s32[]{:S(2)}) async-start(), calls=%async_computation.2 | async-start | bytes 2162688 | tf_op jit(solution)/shard_map/reduce_scatter | solution.py:52
  8.7 4.6 copy-start.5
  102.8 8.9 %copy-start.3 = (bf16[320,256]{1,0:T(8,128)(2,1)S(1)}, bf16[320,256]{1,0:T(8,128)(2,1)}, u32[]{:S(2)}) copy-start(bf16[320,256]{1,0:T(8,128)(2,1)} %param.14) | copy-start | bytes 491524
  113.8 220.9 %copy-start.8 = (f32[256]{0:T(256)S(1)}, f32[256]{0:T(256)}, u32[]{:S(2)}) copy-start(f32[256]{0:T(256)} %param.15) | copy-start | bytes 3076
  113.8 222.6 %copy-start.10 = (s32[512]{0:T(512)S(1)}, s32[512]{0:T(512)}, u32[]{:S(2)}) copy-start(s32[512]{0:T(512)} %param.16) | copy-start | bytes 6148
  113.8 222.7 %copy-start.7 = (s32[64,8]{0,1:T(8,128)S(1)}, s32[64,8]{0,1:T(8,128)}, u32[]{:S(2)}) copy-start(s32[64,8]{0,1:T(8,128)} %param.17) | copy-start | bytes 6148
  113.8 222.7 %copy-start.9 = (s32[64]{0:T(128)S(1)}, s32[64]{0:T(128)}, u32[]{:S(2)}) copy-start(s32[64]{0:T(128)} %param.18) | copy-start | bytes 772
  113.8 298.4 %all-gather.3.cloned.1.call-start = ((), (), s32[]{:S(2)}) async-start(), calls=%async_computation.3 | async-start | bytes 1081344 | tf_op jit(solution)/shard_map/all_gather | solution.py:54
  336.2 339.6 %reduce-scatter.5.cloned.1.call-start = ((), (), s32[]{:S(2)}) async-start(), calls=%async_computation.4 | async-start | bytes 1081344 | tf_op jit(solution)/shard_map/reduce_scatter | solution.py:78
  412.2 3.9 copy-start.1
  415.9 7.2 collective-permute-start
  417.3 23.8 %copy-start.4 = (bf16[64,256]{1,0:T(8,128)(2,1)S(1)}, bf16[64,256]{1,0:T(8,128)(2,1)}, u32[]{:S(2)}) copy-start(bf16[64,256]{1,0:T(8,128)(2,1)} %multiply_convert_fusion.3) | copy-start | bytes 98308
  426.0 15.4 %copy-start.6 = (bf16[64,256]{1,0:T(8,128)(2,1)S(1)}, bf16[64,256]{1,0:T(8,128)(2,1)}, u32[]{:S(2)}) copy-start(bf16[64,256]{1,0:T(8,128)(2,1)} %param.21) | copy-start | bytes 98308
  426.0 15.4 %copy-start.11 = (bf16[1024,256]{1,0:T(8,128)(2,1)S(1)}, bf16[1024,256]{1,0:T(8,128)(2,1)}, u32[]{:S(2)}) copy-start(bf16[1024,256]{1,0:T(8,128)(2,1)} %param.20) | copy-start | bytes 1572868
  448.0 3.9 collective-permute-start.1
  457.9 217.8 %copy-start.2 = (f32[64,256]{1,0:T(8,128)S(1)}, f32[64,256]{1,0:T(8,128)}, u32[]{:S(2)}) copy-start(f32[64,256]{1,0:T(8,128)} %reduce-scatter.3.cloned.1.call-done) | copy-start | bytes 196612
  460.7 292.5 %all-gather.5.cloned.1.call-start = ((), (), s32[]{:S(2)}) async-start(), calls=%async_computation.5 | async-start | bytes 1081344 | tf_op jit(solution)/shard_map/all_gather | solution.py:84
  677.2 142.9 %all-reduce.2.cloned.1.call-start = ((), (), s32[]{:S(2)}) async-start(), calls=%async_computation.6 | async-start | bytes 655360 | tf_op jit(solution)/shard_map/psum | solution.py:88
Sparse Core Ops, SparseCore 0:
  113.9 220.6 reduce-scatter.2
  337.8 74.3 all-gather.2
  460.8 214.9 reduce-scatter.4
  678.8 74.3 all-gather.4
  755.9 64.2 all-reduce.1
where the time goes:
time: 830 us; the launch traced here: 828 us
  waiting for transfers between devices  658 us (79%)
  local copies, waits for them, and re-layouts  123 us (15%)
  other arithmetic  27.3 us (3%)
  between operations  14 us (2%)
    reduce_scatter x1, waiting for transfers between devices, body(): lax.psum_scatter(partial_value, 'feat', scatter_dimension=0, tiled=True)  221 us
    reduce_scatter x1, waiting for transfers between devices, body(): lax.psum_scatter(table_grad.astype(jnp.bfloat16), 'feat', scatter_dimensi...  215 us
    gather x16, local copies, waits for them, and re-layouts, mean_rows(): picked = table[nbrs[:, slot]].astype(jnp.float32)  107 us
    all_gather x1, waiting for transfers between devices, body(): grad_pre_first = lax.all_gather(grad_pre_own, 'feat', axis=0, tiled=True)  75.9 us
    all_gather x1, waiting for transfers between devices, body(): table = lax.all_gather(hidden_own, 'feat', axis=0, tiled=True)  75.6 us
    psum x1, waiting for transfers between devices, body(): grad_first = lax.psum(slice_grad, 'dp')  63.6 us
  transfers between devices with their start and end apart: 7, of which 7 were waited for; matrix products, arithmetic and copies ran while one was open for 1% of the time, Pallas kernels for 0%

commit v1 on v0

--- a/solution.py
+++ b/solution.py
@@ -85,7 +85,11 @@
     slice_grad = lax.dot_general(
         agg_first, grad_pre_first, (((0,), (0,)), ((), ())), preferred_element_type=jnp.float32
     )
-    grad_first = lax.psum(slice_grad, "dp")
+    grad_first = slice_grad
+    for hop in (1, 2, 4):
+        grad_first = grad_first + lax.ppermute(
+            grad_first, "dp", [(dev, dev ^ hop) for dev in range(8)]
+        )
     return (embed, grad_first)
 
 

time: 830 us -> 787 us (0.948)
  waiting for transfers between devices: 658 us -> 611 us
    psum x1 -> x0, waiting for transfers between devices: 63.6 us -> none  [body(): grad_first = lax.psum(slice_grad, 'dp')]
    ppermute x0 -> x3, waiting for transfers between devices: none -> 16.5 us  [body(): lax.ppermute(grad_first, 'dp', [(dev, dev ^ hop) for dev in range(8)])]
  transfers between devices with their start and end apart: 7 -> 9, of which waited for: 7 -> 9; matrix products, arithmetic and copies ran while one was open for 1% -> 1% of each run, Pallas kernels for 0% -> 0%
where the time goes in v1:
time: 787 us; the launch traced here: 784 us
  waiting for transfers between devices  611 us (78%)
  local copies, waits for them, and re-layouts  121 us (15%)
  other arithmetic  28.1 us (4%)
  between operations  14 us (2%)
    reduce_scatter x1, waiting for transfers between devices, body(): lax.psum_scatter(partial_value, 'feat', scatter_dimension=0, tiled=True)  221 us
    reduce_scatter x1, waiting for transfers between devices, body(): lax.psum_scatter(table_grad.astype(jnp.bfloat16), 'feat', scatter_dimensi...  215 us
    gather x16, local copies, waits for them, and re-layouts, mean_rows(): picked = table[nbrs[:, slot]].astype(jnp.float32)  106 us
    all_gather x1, waiting for transfers between devices, body(): grad_pre_first = lax.all_gather(grad_pre_own, 'feat', axis=0, tiled=True)  76.1 us
    all_gather x1, waiting for transfers between devices, body(): table = lax.all_gather(hidden_own, 'feat', axis=0, tiled=True)  75.6 us
    ppermute x3, waiting for transfers between devices, body(): lax.ppermute(grad_first, 'dp', [(dev, dev ^ hop) for dev in range(8)])  16.5 us
  transfers between devices with their start and end apart: 9, of which 9 were waited for; matrix products, arithmetic and copies ran while one was open for 1% of the time, Pallas kernels for 0%

profile of v1, /device:TPU:8, one launch (start us, length us, event | category | flops | bytes accessed | tf_op | source)
XLA Modules:
  0.0 784.5 jit_solution(14976294516062658510)
XLA Ops:
  7.2 0.0 copy-start
  7.2 0.0 reduce-scatter.3.cloned.1.call-start
  7.2 0.8 broadcast_compare_fusion.7
  8.0 0.7 convert_element_type.107
  8.7 4.6 copy.22
  13.3 0.1 compare_select_fusion.7
  13.4 11.1 %gather_fusion = bf16[2048,320]{1,0:T(8,128)(2,1)} fusion(bf16[4096,320]{1,0:T(8,128)(2,1)} %copy.22, s32[2048]{0:T(1024)S(1)} %broadcast_clamp_fusion.7), kind=kCustom, calls=%fused_computation | custom fusion | bytes 2629632 | tf_op jit(solution)/shard_map/gather | solution.py:20
  24.5 11.1 %gather_fusion.1 = bf16[2048,320]{1,0:T(8,128)(2,1)} fusion(bf16[4096,320]{1,0:T(8,128)(2,1)} %copy.22, s32[2048]{0:T(1024)S(1)} %broadcast_clamp_fusion.6), kind=kCustom, calls=%fused_computation.1 | custom fusion | bytes 2629632 | tf_op jit(solution)/shard_map/gather | solution.py:20
  35.7 11.2 %gather_fusion.2 = bf16[2048,320]{1,0:T(8,128)(2,1)} fusion(bf16[4096,320]{1,0:T(8,128)(2,1)} %copy.22, s32[2048]{0:T(1024)S(1)} %broadcast_clamp_fusion.5), kind=kCustom, calls=%fused_computation.2 | custom fusion | bytes 2629632 | tf_op jit(solution)/shard_map/gather | solution.py:20
  46.8 11.2 %gather_fusion.3 = bf16[2048,320]{1,0:T(8,128)(2,1)} fusion(bf16[4096,320]{1,0:T(8,128)(2,1)} %copy.22, s32[2048]{0:T(1024)S(1)} %broadcast_clamp_fusion.4), kind=kCustom, calls=%fused_computation.3 | custom fusion | bytes 2629632 | tf_op jit(solution)/shard_map/gather | solution.py:20
  58.0 11.2 %gather_fusion.4 = bf16[2048,320]{1,0:T(8,128)(2,1)} fusion(bf16[4096,320]{1,0:T(8,128)(2,1)} %copy.22, s32[2048]{0:T(1024)S(1)} %broadcast_clamp_fusion.3), kind=kCustom, calls=%fused_computation.4 | custom fusion | bytes 2629632 | tf_op jit(solution)/shard_map/gather | solution.py:20
  69.2 11.1 %gather_fusion.5 = bf16[2048,320]{1,0:T(8,128)(2,1)} fusion(bf16[4096,320]{1,0:T(8,128)(2,1)} %copy.22, s32[2048]{0:T(1024)S(1)} %broadcast_clamp_fusion.2), kind=kCustom, calls=%fused_computation.5 | custom fusion | bytes 2629632 | tf_op jit(solution)/shard_map/gather | solution.py:20
  80.3 11.1 %gather_fusion.6 = bf16[2048,320]{1,0:T(8,128)(2,1)} fusion(bf16[4096,320]{1,0:T(8,128)(2,1)} %copy.22, s32[2048]{0:T(1024)S(1)} %broadcast_clamp_fusion.1), kind=kCustom, calls=%fused_computation.6 | custom fusion | bytes 2629632 | tf_op jit(solution)/shard_map/gather | solution.py:20
  91.5 11.2 %gather_fusion.7 = bf16[2048,320]{1,0:T(8,128)(2,1)} fusion(bf16[4096,320]{1,0:T(8,128)(2,1)} %copy.22, s32[2048]{0:T(1024)S(1)} %broadcast_clamp_fusion), kind=kCustom, calls=%fused_computation.7 | custom fusion | bytes 2629632 | tf_op jit(solution)/shard_map/gather | solution.py:20
  102.6 8.9 %add_convert_fusion = bf16[2048,320]{1,0:T(8,128)(2,1)S(1)} fusion(bf16[2048,320]{1,0:T(8,128)(2,1)} %gather_fusion.7, bf16[2048,320]{1,0:T(8,128)(2,1)} %gather_fusion.6, bf16[2048,320]{1,0:T(8,128)(2,1)} %gather_fusion.5, bf16[2048,320]{1,0:T(8,128)(2,1)} %gather_fusion.4, bf16[2048,320]{1,0:T(8,128)(2,1)} %gather_fusion.3, ...), kind=kLoop, calls=%fused_computation.19 | loop fusion | flops 17694720 | bytes 13131776 | tf_op jit(solution)/shard_map/convert_element_type | solution.py:50
  111.6 2.0 fusion.40
  113.6 0.0 reduce-scatter.3.cloned.1.call-update
  113.6 0.0 all-gather.3.cloned.1.call-start
  113.7 220.8 %reduce-scatter.3.cloned.1.call-done = f32[64,256]{1,0:T(8,128)} async-done(((f32[2048,256]{1,0:T(8,128)}), f32[64,256]{1,0:T(8,128)}) %reduce-scatter.3.cloned.1.call-update) | async-done | bytes 65552 | tf_op jit(solution)/shard_map/reduce_scatter | solution.py:52
  334.5 1.5 multiply_convert_fusion.3
  336.0 0.0 all-gather.3.cloned.1.call-update
  336.0 0.2 reduce-scatter.5.cloned.1.call-start
  336.4 0.1 fusion.28
  336.5 75.6 %all-gather.3.cloned.1.call-done = bf16[2048,256]{1,0:T(8,128)(2,1)} async-done(((bf16[64,256]{1,0:T(8,128)(2,1)}), bf16[2048,256]{1,0:T(8,128)(2,1)}) %all-gather.3.cloned.1.call-update) | async-done | bytes 1048592 | tf_op jit(solution)/shard_map/all_gather | solution.py:54
  412.1 3.6 gather_fusion.8
  415.7 0.1 copy.31
  415.8 0.1 select_n.163
  415.9 0.1 reshape.203
  416.0 1.1 constant_dynamic-update-slice_fusion.1
  417.1 5.8 collective-permute-done
  422.9 0.7 constant_dynamic-update-slice_fusion
  423.6 2.1 gather_fusion.10
  425.8 0.0 copy-start.6
  425.8 2.2 gather_fusion.11
  428.0 2.1 gather_fusion.12
  430.1 2.1 gather_fusion.13
  432.3 2.1 gather_fusion.14
  434.4 2.1 gather_fusion.15
  436.6 2.1 gather_fusion.9
  438.7 2.1 gather_fusion.16
  440.9 0.3 fusion.16
  441.2 0.5 fusion.3
  441.7 5.1 scatter_custom_fusion
  446.8 1.1 slice.132
  447.8 0.0 collective-permute-start.1
  447.9 3.1 slice.112
  451.0 0.8 collective-permute-done.1
  451.7 6.0 scatter_custom_fusion.1
  457.7 2.7 convert_element_type.125
  460.5 0.0 reduce-scatter.5.cloned.1.call-update
  460.5 0.0 all-gather.5.cloned.1.call-start
  460.5 215.1 %reduce-scatter.5.cloned.1.call-done = bf16[64,256]{1,0:T(8,128)(2,1)} async-done(((bf16[2048,256]{1,0:T(8,128)(2,1)}), bf16[64,256]{1,0:T(8,128)(2,1)}) %reduce-scatter.5.cloned.1.call-update) | async-done | bytes 32784 | tf_op jit(solution)/shard_map/reduce_scatter | solution.py:78
  675.7 1.4 multiply_convert_fusion.2
  677.1 0.0 all-gather.5.cloned.1.call-update
  677.1 76.1 %all-gather.5.cloned.1.call-done = bf16[2048,256]{1,0:T(8,128)(2,1)} async-done(((bf16[64,256]{1,0:T(8,128)(2,1)}), bf16[2048,256]{1,0:T(8,128)(2,1)}) %all-gather.5.cloned.1.call-update) | async-done | bytes 1048592 | tf_op jit(solution)/shard_map/all_gather | solution.py:84
  753.2 1.8 fusion.41
  755.0 0.1 collective-permute-start.2
  755.1 1.6 collective-permute-done.2
  756.8 1.6 collective-permute-start.3
  758.4 8.3 %collective-permute-done.3 = f32[320,256]{1,0:T(8,128)S(1)} collective-permute-done((f32[320,256]{1,0:T(8,128)S(1)}, f32[320,256]{1,0:T(8,128)S(1)}, u32[]{:S(2)}, u32[]{:S(2)}) %collective-permute-start.3) | collective-permute-done | bytes 327712 | tf_op jit(solution)/shard_map/ppermute | solution.py:90
  766.7 3.1 collective-permute-start.4
  769.7 0.8 fusion.4
  770.6 6.6 collective-permute-done.4
  777.2 0.8 add.210
  (43 shorter events, 0.2 us)
Async XLA Ops:
  7.2 433.7 %copy-start = (bf16[256,1024]{1,0:T(8,128)(2,1)S(1)}, bf16[256,1024]{1,0:T(8,128)(2,1)}, u32[]{:S(2)}) copy-start(bf16[256,1024]{1,0:T(8,128)(2,1)} %param.19) | copy-start | bytes 1572868
  7.2 327.3 %reduce-scatter.3.cloned.1.call-start = ((), (), s32[]{:S(2)}) async-start(), calls=%async_computation.2 | async-start | bytes 2162688 | tf_op jit(solution)/shard_map/reduce_scatter | solution.py:52
  8.7 4.6 copy-start.5
  102.6 8.9 %copy-start.3 = (bf16[320,256]{1,0:T(8,128)(2,1)S(1)}, bf16[320,256]{1,0:T(8,128)(2,1)}, u32[]{:S(2)}) copy-start(bf16[320,256]{1,0:T(8,128)(2,1)} %param.14) | copy-start | bytes 491524
  113.6 220.9 %copy-start.8 = (f32[256]{0:T(256)S(1)}, f32[256]{0:T(256)}, u32[]{:S(2)}) copy-start(f32[256]{0:T(256)} %param.15) | copy-start | bytes 3076
  113.6 222.6 %copy-start.10 = (s32[512]{0:T(512)S(1)}, s32[512]{0:T(512)}, u32[]{:S(2)}) copy-start(s32[512]{0:T(512)} %param.16) | copy-start | bytes 6148
  113.6 222.7 %copy-start.7 = (s32[64,8]{0,1:T(8,128)S(1)}, s32[64,8]{0,1:T(8,128)}, u32[]{:S(2)}) copy-start(s32[64,8]{0,1:T(8,128)} %param.17) | copy-start | bytes 6148
  113.6 222.7 %copy-start.9 = (s32[64]{0:T(128)S(1)}, s32[64]{0:T(128)}, u32[]{:S(2)}) copy-start(s32[64]{0:T(128)} %param.18) | copy-start | bytes 772
  113.6 298.4 %all-gather.3.cloned.1.call-start = ((), (), s32[]{:S(2)}) async-start(), calls=%async_computation.3 | async-start | bytes 1081344 | tf_op jit(solution)/shard_map/all_gather | solution.py:54
  336.0 339.7 %reduce-scatter.5.cloned.1.call-start = ((), (), s32[]{:S(2)}) async-start(), calls=%async_computation.4 | async-start | bytes 1081344 | tf_op jit(solution)/shard_map/reduce_scatter | solution.py:78
  412.1 3.9 copy-start.1
  415.7 7.2 collective-permute-start
  417.1 23.8 %copy-start.4 = (bf16[64,256]{1,0:T(8,128)(2,1)S(1)}, bf16[64,256]{1,0:T(8,128)(2,1)}, u32[]{:S(2)}) copy-start(bf16[64,256]{1,0:T(8,128)(2,1)} %multiply_convert_fusion.3) | copy-start | bytes 98308
  425.8 15.4 %copy-start.6 = (bf16[64,256]{1,0:T(8,128)(2,1)S(1)}, bf16[64,256]{1,0:T(8,128)(2,1)}, u32[]{:S(2)}) copy-start(bf16[64,256]{1,0:T(8,128)(2,1)} %param.21) | copy-start | bytes 98308
  425.8 15.4 %copy-start.11 = (bf16[1024,256]{1,0:T(8,128)(2,1)S(1)}, bf16[1024,256]{1,0:T(8,128)(2,1)}, u32[]{:S(2)}) copy-start(bf16[1024,256]{1,0:T(8,128)(2,1)} %param.20) | copy-start | bytes 1572868
  447.8 3.9 collective-permute-start.1
  457.7 217.9 %copy-start.2 = (f32[64,256]{1,0:T(8,128)S(1)}, f32[64,256]{1,0:T(8,128)}, u32[]{:S(2)}) copy-start(f32[64,256]{1,0:T(8,128)} %reduce-scatter.3.cloned.1.call-done) | copy-start | bytes 196612
  460.5 292.7 %all-gather.5.cloned.1.call-start = ((), (), s32[]{:S(2)}) async-start(), calls=%async_computation.5 | async-start | bytes 1081344 | tf_op jit(solution)/shard_map/all_gather | solution.py:84
  755.0 1.7 collective-permute-start.2
  756.8 9.8 %collective-permute-start.3 = (f32[320,256]{1,0:T(8,128)S(1)}, f32[320,256]{1,0:T(8,128)S(1)}, u32[]{:S(2)}, u32[]{:S(2)}) collective-permute-start(f32[320,256]{1,0:T(8,128)S(1)} %add.208), channel_id=1, source_target_pairs={{0,2},{1,3},{2,0},{3,1},{4,6},{5,7},{6,4},{7,5},{8,10},{9,11},{10,... | collective-permute-start | bytes 983048 | tf_op jit(solution)/shard_map/ppermute | solution.py:90
  766.7 10.5 %collective-permute-start.4 = (f32[320,256]{1,0:T(8,128)S(1)}, f32[320,256]{1,0:T(8,128)S(1)}, u32[]{:S(2)}, u32[]{:S(2)}) collective-permute-start(f32[320,256]{1,0:T(8,128)S(1)} %add.209), channel_id=1, source_target_pairs={{0,4},{1,5},{2,6},{3,7},{4,0},{5,1},{6,2},{7,3},{8,12},{9,13},{10,... | collective-permute-start | bytes 983048 | tf_op jit(solution)/shard_map/ppermute | solution.py:90
Sparse Core Ops, SparseCore 0:
  113.8 220.6 reduce-scatter.2
  337.6 74.3 all-gather.2
  460.6 215.0 reduce-scatter.4
  678.7 74.4 all-gather.4
